TPU v7x, 32 devices: a whole 2x2x4 slice. The times are simulated.
32 devices in a mesh: gx: 4 (over z), gy: 4 (over y, x), gz: 2 (over core).
Axes of the slice: x: 2, y: 2, z: 4, core: 2. Of those that a mesh axis runs over, the one named last changes fastest.
Arguments:
- rock_ids: int32 [16, 512, 512], P('gz', 'gx', 'gy'), may hold values from 0 to 7
- log_perm: float32 [16, 512, 512], P('gz', 'gx', 'gy'), may hold values from -3 to 3
- rock_diagonal: float32 [8, 3], replicated, may hold values from 0.2 to 5
- rock_shear: float32 [8, 3], replicated, may hold values from -0.8 to 0.8
- rock_storage: float32 [8], replicated, may hold values from 0.05 to 0.5
- source: float32 [16, 512, 512], P('gz', 'gx', 'gy'), may hold values from -6 to 6
- pressure_start: float32 [16, 512, 512], P('gz', 'gx', 'gy'), may hold values from -6 to 6
Outputs:
- pressure: float32 [16, 512, 512], P('gz', 'gx', 'gy')
- residual: float32 [16, 512, 512], P('gz', 'gx', 'gy')
All inputs are finite; a program needn't handle non-finite values.
Results may differ from a plain program's by a relative error of at most 0.0003.
Values sent between devices are 32-bit elements; how exact they have to be, the bound alone decides.
A program may use at most 128 MiB of HBM per device.

v0:
```python
import itertools

import jax
import jax.numpy as jnp
from jax import lax
from jax.experimental import pallas as pl
from jax.experimental.pallas import tpu as pltpu
from jax.sharding import PartitionSpec as P

ITERS = 2
SWEEPS = 2
ROBIN = 0.5
AXES = ("gz", "gx", "gy")
LANES = 128


def build_offsets():
    found = []
    for axis in range(3):
        for sign in (1, -1):
            vector = [0, 0, 0]
            vector[axis] = sign
            found.append((tuple(vector), axis, 1))
    for first, second, comp in ((0, 1, 3), (0, 2, 4), (1, 2, 5)):
        for sign_a in (1, -1):
            for sign_b in (1, -1):
                vector = [0, 0, 0]
                vector[first] = sign_a
                vector[second] = sign_b
                found.append((tuple(vector), comp, sign_a * sign_b))
    return found


OFFSETS = build_offsets()
DIRS = [vector for vector, comp, sign in OFFSETS]
SLOT = {vector: index for index, vector in enumerate(DIRS)}
X_DIRS = [d for d in DIRS if d[1] != 0]
Y_DIRS = [d for d in DIRS if d[1] == 0 and d[2] != 0]
Z_DIRS = [d for d in DIRS if d[1] == 0 and d[2] == 0]
X_SLOT = {d: i for i, d in enumerate(X_DIRS)}
Y_SLOT = {d: i for i, d in enumerate(Y_DIRS)}
Z_SLOT = {d: i for i, d in enumerate(Z_DIRS)}


def make_kernel(sizes, shape, classes):
    cz, cx, cy = shape
    tiles = cx // 8
    top = cx + 8
    last = cz - 1

    def kernel(
        ids_ref, lp_ref, dia_ref, she_ref, sto_ref, src_ref, p_ref,
        out_ref, res_ref,
        tab, ten, ten_h, ten_p, ten_m, stor,
        va, vap, vam, vb, vbp, vbm, vh,
        coef, diag, robin, inv, base, pack,
        zs1, xs1, ys1, zl1, xl1, yl1,
        zs2, xs2, ys2, zl2, xl2, yl2,
        zs3, xs3, ys3, zl3, xl3, yl3,
        send_sem, recv_sem,
    ):
        here = [lax.axis_index(a) for a in AXES]

        def exists(d):
            ok = None
            for axis in range(3):
                if d[axis] == 1:
                    term = here[axis] < sizes[axis] - 1
                elif d[axis] == -1:
                    term = here[axis] > 0
                else:
                    continue
                ok = term if ok is None else jnp.logical_and(ok, term)
            return ok

        def target(d):
            return {a: here[i] + d[i] for i, a in enumerate(AXES) if d[i] != 0}

        there = {d: exists(d) for d in DIRS}
        barrier = pltpu.get_barrier_semaphore()

        for ref in (zl1, xl1, yl1, zl2, xl2, yl2, zl3, xl3, yl3):
            ref[...] = jnp.zeros_like(ref)

        expected = jnp.int32(0)
        for d in DIRS:
            @pl.when(there[d])
            def _(d=d):
                pl.semaphore_signal(
                    barrier, inc=1, device_id=target(d),
                    device_id_type=pl.DeviceIdType.MESH,
                )
            expected = expected + there[d].astype(jnp.int32)

        stages = (
            (zs1, xs1, ys1, zl1, xl1, yl1),
            (zs2, xs2, ys2, zl2, xl2, yl2),
            (zs3, xs3, ys3, zl3, xl3, yl3),
        )

        lane = lax.broadcasted_iota(jnp.int32, (cx, LANES), 1)

        def pack_faces(stage, q, plane, row):
            zs, xs, ys = stages[stage][:3]
            for side, z in ((0, 0), (1, last)):
                zs[side, q] = plane(z)
            for side, x in ((0, 0), (1, cx - 1)):
                xs[side, q] = row(x)
            mixed = jnp.zeros((cx, LANES), jnp.float32)
            for z in range(cz):
                moved = pltpu.roll(plane(z), 2 * z + 1, 1)
                mixed = jnp.where((lane // 2) == z, moved, mixed)
            ys[q] = mixed.T[: 2 * cz]

        def copy_of(stage, d):
            zs, xs, ys, zl, xl, yl = stages[stage]
            if d[1] != 0:
                src, dst = xs.at[(d[1] + 1) // 2], xl.at[X_SLOT[d]]
            elif d[2] != 0:
                src, dst = ys, yl.at[Y_SLOT[d]]
            else:
                src, dst = zs.at[(d[0] + 1) // 2], zl.at[Z_SLOT[d]]
            return pltpu.make_async_remote_copy(
                src_ref=src, dst_ref=dst,
                send_sem=send_sem.at[stage, SLOT[d]],
                recv_sem=recv_sem.at[stage, SLOT[d]],
                device_id=target(d), device_id_type=pl.DeviceIdType.MESH,
            )

        def opposite(d):
            return tuple(-c for c in d)

        def start(stage):
            for d in DIRS:
                @pl.when(there[d])
                def _(d=d):
                    copy_of(stage, d).start()

        def arrive(stage):
            for d in DIRS:
                @pl.when(there[opposite(d)])
                def _(d=d):
                    copy_of(stage, d).wait_recv()

        def getters(stage, q):
            zl, xl, yl = stages[stage][3:]

            def get_z(sz):
                return zl[Z_SLOT[(-sz, 0, 0)], q]

            def get_x(sx, sz, sy):
                return xl[X_SLOT[(-sz, -sx, -sy)], q]

            def get_y(sy, sz):
                return yl[Y_SLOT[(-sz, 0, -sy)], q]

            return get_z, get_x, get_y

        lane8 = lax.broadcasted_iota(jnp.int32, (cz, LANES), 1)
        even = lax.broadcasted_iota(jnp.int32, (2 * cz, LANES), 0) % 2 == 0

        def fill_center(field, get, has_z, has_x):
            get_z, get_x, get_y = get
            if has_z:
                for sz, z in ((-1, 0), (1, cz + 1)):
                    field[z, 8:top, :] = get_z(sz)
            if has_x:
                for sx, row in ((-1, 7), (1, top)):
                    field[1 : cz + 1, row, :] = get_x(sx, 0, 0)
                    if has_z:
                        field[0, row, :] = get_x(sx, -1, 0)[last]
                        field[cz + 1, row, :] = get_x(sx, 1, 0)[0]

        def fill_side(hold, get, has_z, has_x):
            get_z, get_x, get_y = get
            if has_x:
                for sx, row in ((-1, 7), (1, top)):
                    hold[1 : cz + 1, row, :] = jnp.where(
                        lane8 >= LANES // 2, get_x(sx, 0, -1), get_x(sx, 0, 1)
                    )
            pack[0 : 2 * cz, :] = jnp.where(even, get_y(-1, 0), get_y(1, 0))
            if has_z:
                pack[2 * cz : 4 * cz, :] = jnp.where(even, get_y(-1, -1), get_y(1, -1))
                pack[4 * cz : 6 * cz, :] = jnp.where(even, get_y(-1, 1), get_y(1, 1))
            turned = pack[...].T
            for z in range(cz):
                hold[z + 1, 8:top, :] = pltpu.roll(turned, LANES - 1 - 2 * z, 1)
            if has_z:
                hold[0, 8:top, :] = pltpu.roll(turned, LANES - 1 - (4 * cz - 2), 1)
                hold[cz + 1, 8:top, :] = pltpu.roll(turned, LANES - 1 - 4 * cz, 1)

        def shift_pair(value, side):
            spot = lax.broadcasted_iota(jnp.int32, value.shape, value.ndim - 1)
            ahead = pltpu.roll(jnp.where(spot == 0, side, value), LANES - 1, value.ndim - 1)
            behind = pltpu.roll(jnp.where(spot == LANES - 1, side, value), 1, value.ndim - 1)
            return ahead, behind

        pack_faces(
            0, 0,
            lambda z: (ids_ref[z] + 1).astype(jnp.float32),
            lambda x: (ids_ref[:, x, :] + 1).astype(jnp.float32),
        )
        pack_faces(0, 1, lambda z: lp_ref[z], lambda x: lp_ref[:, x, :])
        pack_faces(0, 2, lambda z: p_ref[z], lambda x: p_ref[:, x, :])

        pl.semaphore_wait(barrier, expected)
        start(0)

        for c in range(classes):
            cols = [jnp.full((8, LANES), dia_ref[c, k], jnp.float32) for k in range(3)]
            for k in range(3):
                tab[k, c] = cols[k]
            for k, (a, b) in enumerate(((0, 1), (0, 2), (1, 2))):
                tab[3 + k, c] = she_ref[c, k] * jnp.sqrt(cols[a] * cols[b])
            tab[6, c] = jnp.full((8, LANES), sto_ref[c], jnp.float32)

        def rows_of(t):
            return pl.ds(pl.multiple_of(t * 8, 8), 8)

        def lookup(code, comps):
            found = [jnp.zeros(code.shape, jnp.float32) for _ in comps]
            for c in range(classes):
                hit = code == jnp.float32(c + 1)
                found = [
                    jnp.where(hit, jnp.broadcast_to(tab[k, c, 0:1, :], code.shape), f)
                    for k, f in zip(comps, found)
                ]
            return found

        def tensor_tile(t, carry):
            r = rows_of(t)
            out = rows_of(t + 1)
            code = (ids_ref[:, r, :] + 1).astype(jnp.float32)
            gain = jnp.exp(lp_ref[:, r, :])
            found = lookup(code, range(7))
            for k in range(6):
                ten[k, 1 : cz + 1, out, :] = found[k] * gain
            stor[:, r, :] = found[6]
            va[1 : cz + 1, out, :] = p_ref[:, r, :]
            return carry

        lax.fori_loop(0, tiles, tensor_tile, 0)

        arrive(0)

        gid = getters(0, 0)
        glp = getters(0, 1)

        def tensor_get(k):
            def of(which):
                def get(*args):
                    code = gid[which](*args)
                    return lookup(code, [k])[0] * jnp.exp(glp[which](*args))
                return get
            return of(0), of(1), of(2)

        fill_center(ten.at[0], tensor_get(0), True, False)
        fill_center(ten.at[1], tensor_get(1), False, True)
        fill_center(ten.at[3], tensor_get(3), True, True)
        fill_center(ten.at[4], tensor_get(4), True, False)
        fill_center(ten.at[5], tensor_get(5), False, True)
        fill_side(ten_h.at[0], tensor_get(2), False, False)
        fill_side(ten_h.at[1], tensor_get(4), True, False)
        fill_side(ten_h.at[2], tensor_get(5), False, True)

        def tensor_shift(t, carry):
            r = rows_of(t)
            for slot, k in ((0, 2), (1, 4), (2, 5)):
                ahead, behind = shift_pair(ten[k, :, r, :], ten_h[slot, :, r, :])
                ten_p[slot, :, r, :] = ahead
                ten_m[slot, :, r, :] = behind
            return carry

        lax.fori_loop(0, tiles + 2, tensor_shift, 0)

        def load_halo(stage, q):
            get = getters(stage, q)
            fill_center(va, get, True, True)
            fill_side(vh, get, True, True)

            def shift(t, carry):
                r = rows_of(t)
                value = va[:, r, :]
                ahead, behind = shift_pair(value, vh[:, r, :])
                vap[:, r, :] = ahead
                vam[:, r, :] = behind
                for ref, got in ((vb, value), (vbp, ahead), (vbm, behind)):
                    ref[0, r, :] = got[0]
                    ref[cz + 1, r, :] = got[cz + 1]
                return carry

            lax.fori_loop(0, tiles + 2, shift, 0)
            for source, dest in ((va, vb), (vap, vbp), (vam, vbm)):
                for lo in (0, top):
                    dest[:, lo : lo + 8, :] = source[:, lo : lo + 8, :]

        def near_of(refs, t):
            plain, plus, minus = refs
            by_y = {0: plain, 1: plus, -1: minus}
            cache = {}

            def near(vector):
                dz, dx, dy = vector
                if (dx, dy) not in cache:
                    ref = by_y[dy]
                    r = pl.ds(t * 8 + 8 + dx, 8) if dx else rows_of(t + 1)
                    if dx and dy:
                        cache[(dx, dy)] = ref[1 : cz + 1, r, :]
                    else:
                        cache[(dx, dy)] = ref[:, r, :]
                got = cache[(dx, dy)]
                if dx and dy:
                    return got
                return got[1 + dz : 1 + dz + cz]

            return near

        zi = lax.broadcasted_iota(jnp.int32, (cz, 8, LANES), 0)
        xi = lax.broadcasted_iota(jnp.int32, (cz, 8, LANES), 1)
        yi = lax.broadcasted_iota(jnp.int32, (cz, 8, LANES), 2)

        def coef_tile(t, carry):
            r = rows_of(t)
            mid = rows_of(t + 1)
            at = (zi, xi + t * 8, yi)
            total = stor[:, r, :]
            rim = jnp.zeros((cz, 8, LANES), jnp.float32)
            nears = {
                0: near_of((ten.at[0], None, None), t),
                1: near_of((ten.at[1], None, None), t),
                2: near_of((ten.at[2], ten_p.at[0], ten_m.at[0]), t),
                3: near_of((ten.at[3], None, None), t),
                4: near_of((ten.at[4], ten_p.at[1], ten_m.at[1]), t),
                5: near_of((ten.at[5], ten_p.at[2], ten_m.at[2]), t),
            }
            for e, (vector, comp, sign) in enumerate(OFFSETS):
                own = ten[comp, 1 : cz + 1, mid, :]
                near = nears[comp](vector)
                if comp < 3:
                    value = 2.0 * own * near / (own + near)
                else:
                    value = 0.125 * sign * (own + near)
                coef[e, :, r, :] = value
                size = jnp.abs(value)
                total = total + size
                out = None
                for axis in range(3):
                    if vector[axis] == 0:
                        continue
                    edge = shape[axis] - 1 if vector[axis] == 1 else 0
                    hit = at[axis] == edge
                    out = hit if out is None else jnp.logical_or(out, hit)
                rim = rim + jnp.where(out, size, jnp.float32(0))
            rim = ROBIN * rim
            diag[:, r, :] = total
            robin[:, r, :] = rim
            inv[:, r, :] = 1.0 / (total + rim)
            return carry

        lax.fori_loop(0, tiles, coef_tile, 0)

        def gather(refs, t, acc):
            near = near_of(refs, t)
            r = rows_of(t)
            for e, (vector, comp, sign) in enumerate(OFFSETS):
                acc = acc + coef[e, :, r, :] * near(vector)
            return acc

        a_refs = (va, vap, vam)
        b_refs = (vb, vbp, vbm)

        def first_sweep(t, carry):
            r = rows_of(t)
            mid = rows_of(t + 1)
            steady = src_ref[:, r, :] + robin[:, r, :] * va[1 : cz + 1, mid, :]
            base[:, r, :] = steady
            u = gather(a_refs, t, steady) * inv[:, r, :]
            vb[1 : cz + 1, mid, :] = u
            ahead, behind = shift_pair(u, vh[1 : cz + 1, mid, :])
            vbp[1 : cz + 1, mid, :] = ahead
            vbm[1 : cz + 1, mid, :] = behind
            return carry

        def last_sweep(t, carry):
            r = rows_of(t)
            mid = rows_of(t + 1)
            u = gather(b_refs, t, base[:, r, :]) * inv[:, r, :]
            va[1 : cz + 1, mid, :] = u
            return carry

        for step in range(ITERS):
            load_halo(step, 2 if step == 0 else 0)
            lax.fori_loop(0, tiles, first_sweep, 0)
            lax.fori_loop(0, tiles, last_sweep, 0)
            pack_faces(
                step + 1, 0,
                lambda z: va[z + 1, 8:top, :],
                lambda x: va[1 : cz + 1, 8 + x, :],
            )
            start(step + 1)
            if step == ITERS - 1:
                out_ref[...] = va[1 : cz + 1, 8:top, :]
            arrive(step + 1)
        load_halo(ITERS, 0)

        def residual_tile(t, carry):
            r = rows_of(t)
            mid = rows_of(t + 1)
            applied = src_ref[:, r, :] - diag[:, r, :] * va[1 : cz + 1, mid, :]
            res_ref[:, r, :] = gather(a_refs, t, applied)
            return carry

        lax.fori_loop(0, tiles, residual_tile, 0)

        for stage in range(ITERS + 1):
            for d in DIRS:
                @pl.when(there[d])
                def _(d=d, stage=stage):
                    copy_of(stage, d).wait_send()

    return kernel


def solution(mesh):
    sizes = tuple(mesh.shape[a] for a in AXES)

    def per_device(rock_ids, log_perm, rock_diagonal, rock_shear, rock_storage, source, pressure_start):
        shape = rock_ids.shape
        cz, cx, cy = shape
        classes = rock_storage.shape[0]
        f32 = jnp.float32
        padded = (cz + 2, cx + 16, cy)

        def exchange(nq):
            return [
                pltpu.VMEM((2, nq, cx, cy), f32),
                pltpu.VMEM((2, nq, cz, cy), f32),
                pltpu.VMEM((nq, 2 * cz, cx), f32),
                pltpu.VMEM((len(Z_DIRS), nq, cx, cy), f32),
                pltpu.VMEM((len(X_DIRS), nq, cz, cy), f32),
                pltpu.VMEM((len(Y_DIRS), nq, 2 * cz, cx), f32),
            ]

        vmem = pl.BlockSpec(memory_space=pltpu.VMEM)
        smem = pl.BlockSpec(memory_space=pltpu.SMEM)
        return pl.pallas_call(
            make_kernel(sizes, shape, classes),
            out_shape=(jax.ShapeDtypeStruct(shape, f32), jax.ShapeDtypeStruct(shape, f32)),
            in_specs=[vmem, vmem, smem, smem, smem, vmem, vmem],
            out_specs=(vmem, vmem),
            scratch_shapes=[
                pltpu.VMEM((7, classes, 8, cy), f32),
                pltpu.VMEM((6,) + padded, f32),
                pltpu.VMEM((3,) + padded, f32),
                pltpu.VMEM((3,) + padded, f32),
                pltpu.VMEM((3,) + padded, f32),
                pltpu.VMEM(shape, f32),
            ]
            + [pltpu.VMEM(padded, f32)] * 7
            + [pltpu.VMEM((len(OFFSETS),) + shape, f32)]
            + [pltpu.VMEM(shape, f32)] * 4
            + [pltpu.VMEM((cx, cy), f32)]
            + exchange(3)
            + exchange(1)
            + exchange(1)
            + [
                pltpu.SemaphoreType.DMA((ITERS + 1, len(DIRS))),
                pltpu.SemaphoreType.DMA((ITERS + 1, len(DIRS))),
            ],
            compiler_params=pltpu.CompilerParams(
                collective_id=0, has_side_effects=True, vmem_limit_bytes=60 * 1024 * 1024
            ),
            name="schwarz",
        )(rock_ids, log_perm, rock_diagonal, rock_shear, rock_storage, source, pressure_start)

    block = P("gz", "gx", "gy")
    return jax.shard_map(
        per_device,
        mesh=mesh,
        in_specs=(block, block, P(), P(), P(), block, block),
        out_specs=(block, block),
        check_vma=False,
    )
```

profile of v0, /device:TPU:0, one launch (start us, length us, event | category | flops | bytes accessed | tf_op | source)
XLA Modules:
  0.0 48.0 jit_solution(18226225254564455950)
XLA Ops:
  0.6 0.0 copy-start.1
  0.6 1.4 %copy.9.dia_ref = f32[8,3]{1,0:T(8,128)} copy(f32[8,3]{0,1:T(4,128)} %param.9) | data formatting | bytes 192 | tf_op args[2]
  2.0 0.0 copy-done.1
  2.0 0.7 %copy.10.she_ref = f32[8,3]{1,0:T(8,128)} copy(f32[8,3]{0,1:T(4,128)S(1)} %copy-done.1) | data formatting | bytes 192 | tf_op args[3]
  2.7 42.6 %schwarz.1 = (f32[8,128,128]{2,1,0:T(8,128)}, f32[8,128,128]{2,1,0:T(8,128)}) custom-call(s32[8,128,128]{2,1,0:T(8,128)} %ids_ref.1, f32[8,128,128]{2,1,0:T(8,128)} %lp_ref.1, f32[8,3]{1,0:T(8,128)} %copy.9.dia_ref, f32[8,3]{1,0:T(8,128)} %copy.10.she_ref, f32[8]{0:T(128)} %sto_ref.1, f32[8,128,128]{2,1,0:T(8,128)} %src_ref.1, f32[8,128,128]{2,1,0:T(8,128)} %p_ref.1), custom_call_target="tpu_custom_call" | custom-call | tf_op jit(solution)/shard_map/schwarz/pallas_call | solution.py:446
  45.3 0.0 copy-start
  45.3 1.9 %copy.13 = f32[8,128,128]{2,1,0:T(8,128)} copy(f32[8,128,128]{2,1,0:T(8,128)} %get-tuple-element.4) | data formatting | bytes 1048576
  47.2 0.0 copy-done
  47.2 0.8 %copy.14 = f32[8,128,128]{2,1,0:T(8,128)} copy(f32[8,128,128]{2,1,0:T(8,128)S(1)} %copy-done) | data formatting | bytes 1048576
Async XLA Ops:
  0.6 1.4 %copy-start.1 = (f32[8,3]{0,1:T(4,128)S(1)}, f32[8,3]{0,1:T(4,128)}, u32[]{:S(2)}) copy-start(f32[8,3]{0,1:T(4,128)} %param.10) | copy-start | bytes 292
  45.3 1.9 %copy-start = (f32[8,128,128]{2,1,0:T(8,128)S(1)}, f32[8,128,128]{2,1,0:T(8,128)}, u32[]{:S(2)}) copy-start(f32[8,128,128]{2,1,0:T(8,128)} %get-tuple-element.5) | copy-start | bytes 1572868
where the time goes:
time: 48.2 us; the launch traced here: 48 us
  Pallas kernels  42.6 us (88%)
  local copies, waits for them, and re-layouts  4.76 us (10%)
  between operations  0.66 us (1%)
    pallas_call x1, Pallas kernels, per_device(): pl.pallas_call(make_kernel(sizes, shape, classes), out_shape=(jax.ShapeDt...  42.6 us
    unnamed x8, local copies, waits for them, and re-layouts  4.76 us

commit v1 on v0

--- a/solution.py
+++ b/solution.py
@@ -51,9 +51,10 @@
     def kernel(
         ids_ref, lp_ref, dia_ref, she_ref, sto_ref, src_ref, p_ref,
         out_ref, res_ref,
-        tab, ten, ten_h, ten_p, ten_m, stor,
-        va, vap, vam, vb, vbp, vbm, vh,
-        coef, diag, robin, inv, base, pack,
+        tab, ten, ten_p, ten_m,
+        va, vap, vam, vb, vbp, vbm,
+        coef, diag, robin, inv, base, part, pack, zpad,
+        rcx, rcy, rcz,
         zs1, xs1, ys1, zl1, xl1, yl1,
         zs2, xs2, ys2, zl2, xl2, yl2,
         zs3, xs3, ys3, zl3, xl3, yl3,
@@ -131,7 +132,7 @@
             return tuple(-c for c in d)
 
         def start(stage):
-            for d in DIRS:
+            for d in reversed(DIRS):
                 @pl.when(there[d])
                 def _(d=d):
                     copy_of(stage, d).start()
@@ -156,44 +157,88 @@
 
             return get_z, get_x, get_y
 
-        lane8 = lax.broadcasted_iota(jnp.int32, (cz, LANES), 1)
-        even = lax.broadcasted_iota(jnp.int32, (2 * cz, LANES), 0) % 2 == 0
-
-        def fill_center(field, get, has_z, has_x):
+        lane_x = lax.broadcasted_iota(jnp.int32, (cz, LANES), 1)
+        sub_x = lax.broadcasted_iota(jnp.int32, (cz, LANES), 0)
+        lane_y = lax.broadcasted_iota(jnp.int32, (2 * cz, LANES), 1)
+        sub_y = lax.broadcasted_iota(jnp.int32, (2 * cz, LANES), 0)
+        even = sub_y % 2 == 0
+        zero = jnp.float32(0)
+
+        def turn(value):
+            axis = value.ndim - 1
+            return pltpu.roll(value, LANES - 1, axis), pltpu.roll(value, 1, axis)
+
+        def near_x(get, sx, kinds):
+            get_x = get[1]
+            plain = get_x(sx, 0, 0)
+            out = [plain]
+            if "z" in kinds:
+                out.append(jnp.where(sub_x < last, pltpu.roll(plain, cz - 1, 0), zero))
+                out.append(jnp.where(sub_x > 0, pltpu.roll(plain, 1, 0), zero))
+            if "y" in kinds:
+                side = jnp.where(lane_x >= LANES // 2, get_x(sx, 0, -1), get_x(sx, 0, 1))
+                out.append(pltpu.roll(jnp.where(lane_x == 0, side, plain), LANES - 1, 1))
+                out.append(pltpu.roll(jnp.where(lane_x == LANES - 1, side, plain), 1, 1))
+            return out
+
+        def near_y(get, kinds):
+            get_y = get[2]
+            plain = jnp.where(
+                even,
+                pltpu.roll(get_y(1, 0), 2 * cz - 1, 0),
+                pltpu.roll(get_y(-1, 0), 1, 0),
+            )
+            out = [plain]
+            if "z" in kinds:
+                out.append(jnp.where(sub_y < 2 * last, pltpu.roll(plain, 2 * cz - 2, 0), zero))
+                out.append(jnp.where(sub_y >= 2, pltpu.roll(plain, 2, 0), zero))
+            if "x" in kinds:
+                ahead, behind = turn(plain)
+                out.append(jnp.where(lane_y < LANES - 1, ahead, zero))
+                out.append(jnp.where(lane_y > 0, behind, zero))
+            return out
+
+        def pack_sides(get):
+            get_y = get[2]
+            pack[2 * cz : 4 * cz, :] = jnp.where(even, get_y(-1, -1), get_y(1, -1))
+            pack[4 * cz : 6 * cz, :] = jnp.where(even, get_y(-1, 1), get_y(1, 1))
+
+        def near_z(get, sz, kinds, turned):
             get_z, get_x, get_y = get
-            if has_z:
-                for sz, z in ((-1, 0), (1, cz + 1)):
-                    field[z, 8:top, :] = get_z(sz)
-            if has_x:
-                for sx, row in ((-1, 7), (1, top)):
-                    field[1 : cz + 1, row, :] = get_x(sx, 0, 0)
-                    if has_z:
-                        field[0, row, :] = get_x(sx, -1, 0)[last]
-                        field[cz + 1, row, :] = get_x(sx, 1, 0)[0]
-
-        def fill_side(hold, get, has_z, has_x):
-            get_z, get_x, get_y = get
-            if has_x:
-                for sx, row in ((-1, 7), (1, top)):
-                    hold[1 : cz + 1, row, :] = jnp.where(
-                        lane8 >= LANES // 2, get_x(sx, 0, -1), get_x(sx, 0, 1)
-                    )
-            pack[0 : 2 * cz, :] = jnp.where(even, get_y(-1, 0), get_y(1, 0))
-            if has_z:
-                pack[2 * cz : 4 * cz, :] = jnp.where(even, get_y(-1, -1), get_y(1, -1))
-                pack[4 * cz : 6 * cz, :] = jnp.where(even, get_y(-1, 1), get_y(1, 1))
-            turned = pack[...].T
+            plain = get_z(sz)
+            out = [plain]
+            row = last if sz == -1 else 0
+            if "x" in kinds:
+                zpad[8:top, :] = plain
+                zpad[7:8, :] = get_x(-1, sz, 0)[row : row + 1]
+                zpad[top : top + 1, :] = get_x(1, sz, 0)[row : row + 1]
+                out.append(zpad[9 : top + 1, :])
+                out.append(zpad[7 : top - 1, :])
+            if "y" in kinds:
+                first = 4 * cz - 2 if sz == -1 else 4 * cz
+                side = pltpu.roll(turned, LANES - 1 - first, 1)
+                out.append(pltpu.roll(jnp.where(lane == 0, side, plain), LANES - 1, 1))
+                out.append(pltpu.roll(jnp.where(lane == LANES - 1, side, plain), 1, 1))
+            return out
+
+        def harmonic(own, near):
+            return 2.0 * own * near / (own + near)
+
+        ends = jnp.logical_or(lane == 0, lane == LANES - 1)
+
+        def spread(dest, add, turned, of_x, of_z):
             for z in range(cz):
-                hold[z + 1, 8:top, :] = pltpu.roll(turned, LANES - 1 - 2 * z, 1)
-            if has_z:
-                hold[0, 8:top, :] = pltpu.roll(turned, LANES - 1 - (4 * cz - 2), 1)
-                hold[cz + 1, 8:top, :] = pltpu.roll(turned, LANES - 1 - 4 * cz, 1)
-
-        def shift_pair(value, side):
-            spot = lax.broadcasted_iota(jnp.int32, value.shape, value.ndim - 1)
-            ahead = pltpu.roll(jnp.where(spot == 0, side, value), LANES - 1, value.ndim - 1)
-            behind = pltpu.roll(jnp.where(spot == LANES - 1, side, value), 1, value.ndim - 1)
-            return ahead, behind
+                got = jnp.where(ends, pltpu.roll(turned, LANES - 1 - 2 * z, 1), zero)
+                if z == 0:
+                    got = got + of_z(-1)
+                if z == last:
+                    got = got + of_z(1)
+                if add:
+                    dest[z] += got
+                else:
+                    dest[z] = got
+            for sx, row in ((-1, 0), (1, cx - 1)):
+                dest[:, row, :] += of_x(sx)
 
         pack_faces(
             0, 0,
@@ -203,16 +248,20 @@
         pack_faces(0, 1, lambda z: lp_ref[z], lambda x: lp_ref[:, x, :])
         pack_faces(0, 2, lambda z: p_ref[z], lambda x: p_ref[:, x, :])
 
-        pl.semaphore_wait(barrier, expected)
-        start(0)
-
         for c in range(classes):
-            cols = [jnp.full((8, LANES), dia_ref[c, k], jnp.float32) for k in range(3)]
+            cols = [jnp.full((8, LANES), dia_ref[k, c], jnp.float32) for k in range(3)]
             for k in range(3):
                 tab[k, c] = cols[k]
             for k, (a, b) in enumerate(((0, 1), (0, 2), (1, 2))):
-                tab[3 + k, c] = she_ref[c, k] * jnp.sqrt(cols[a] * cols[b])
+                tab[3 + k, c] = she_ref[k, c] * jnp.sqrt(cols[a] * cols[b])
             tab[6, c] = jnp.full((8, LANES), sto_ref[c], jnp.float32)
+
+        pack[...] = jnp.zeros_like(pack)
+        for ref in (va, vap, vam, vb, vbp, vbm):
+            for z in (0, cz + 1):
+                ref[z] = jnp.zeros_like(ref[z])
+            for lo in (0, top):
+                ref[:, lo : lo + 8, :] = jnp.zeros((cz + 2, 8, LANES), jnp.float32)
 
         def rows_of(t):
             return pl.ds(pl.multiple_of(t * 8, 8), 8)
@@ -234,65 +283,25 @@
             gain = jnp.exp(lp_ref[:, r, :])
             found = lookup(code, range(7))
             for k in range(6):
-                ten[k, 1 : cz + 1, out, :] = found[k] * gain
-            stor[:, r, :] = found[6]
-            va[1 : cz + 1, out, :] = p_ref[:, r, :]
+                value = found[k] * gain
+                ten[k, 1 : cz + 1, out, :] = value
+                if k in (2, 4, 5):
+                    slot = (2, 4, 5).index(k)
+                    ahead, behind = turn(value)
+                    ten_p[slot, 1 : cz + 1, out, :] = ahead
+                    ten_m[slot, 1 : cz + 1, out, :] = behind
+            diag[:, r, :] = found[6]
+            value = p_ref[:, r, :]
+            ahead, behind = turn(value)
+            va[1 : cz + 1, out, :] = value
+            vap[1 : cz + 1, out, :] = ahead
+            vam[1 : cz + 1, out, :] = behind
             return carry
 
         lax.fori_loop(0, tiles, tensor_tile, 0)
 
-        arrive(0)
-
-        gid = getters(0, 0)
-        glp = getters(0, 1)
-
-        def tensor_get(k):
-            def of(which):
-                def get(*args):
-                    code = gid[which](*args)
-                    return lookup(code, [k])[0] * jnp.exp(glp[which](*args))
-                return get
-            return of(0), of(1), of(2)
-
-        fill_center(ten.at[0], tensor_get(0), True, False)
-        fill_center(ten.at[1], tensor_get(1), False, True)
-        fill_center(ten.at[3], tensor_get(3), True, True)
-        fill_center(ten.at[4], tensor_get(4), True, False)
-        fill_center(ten.at[5], tensor_get(5), False, True)
-        fill_side(ten_h.at[0], tensor_get(2), False, False)
-        fill_side(ten_h.at[1], tensor_get(4), True, False)
-        fill_side(ten_h.at[2], tensor_get(5), False, True)
-
-        def tensor_shift(t, carry):
-            r = rows_of(t)
-            for slot, k in ((0, 2), (1, 4), (2, 5)):
-                ahead, behind = shift_pair(ten[k, :, r, :], ten_h[slot, :, r, :])
-                ten_p[slot, :, r, :] = ahead
-                ten_m[slot, :, r, :] = behind
-            return carry
-
-        lax.fori_loop(0, tiles + 2, tensor_shift, 0)
-
-        def load_halo(stage, q):
-            get = getters(stage, q)
-            fill_center(va, get, True, True)
-            fill_side(vh, get, True, True)
-
-            def shift(t, carry):
-                r = rows_of(t)
-                value = va[:, r, :]
-                ahead, behind = shift_pair(value, vh[:, r, :])
-                vap[:, r, :] = ahead
-                vam[:, r, :] = behind
-                for ref, got in ((vb, value), (vbp, ahead), (vbm, behind)):
-                    ref[0, r, :] = got[0]
-                    ref[cz + 1, r, :] = got[cz + 1]
-                return carry
-
-            lax.fori_loop(0, tiles + 2, shift, 0)
-            for source, dest in ((va, vb), (vap, vbp), (vam, vbm)):
-                for lo in (0, top):
-                    dest[:, lo : lo + 8, :] = source[:, lo : lo + 8, :]
+        pl.semaphore_wait(barrier, expected)
+        start(0)
 
         def near_of(refs, t):
             plain, plus, minus = refs
@@ -323,8 +332,7 @@
             r = rows_of(t)
             mid = rows_of(t + 1)
             at = (zi, xi + t * 8, yi)
-            total = stor[:, r, :]
-            rim = jnp.zeros((cz, 8, LANES), jnp.float32)
+            total = diag[:, r, :]
             nears = {
                 0: near_of((ten.at[0], None, None), t),
                 1: near_of((ten.at[1], None, None), t),
@@ -337,12 +345,9 @@
                 own = ten[comp, 1 : cz + 1, mid, :]
                 near = nears[comp](vector)
                 if comp < 3:
-                    value = 2.0 * own * near / (own + near)
+                    value = harmonic(own, near)
                 else:
                     value = 0.125 * sign * (own + near)
-                coef[e, :, r, :] = value
-                size = jnp.abs(value)
-                total = total + size
                 out = None
                 for axis in range(3):
                     if vector[axis] == 0:
@@ -350,48 +355,162 @@
                     edge = shape[axis] - 1 if vector[axis] == 1 else 0
                     hit = at[axis] == edge
                     out = hit if out is None else jnp.logical_or(out, hit)
-                rim = rim + jnp.where(out, size, jnp.float32(0))
+                value = jnp.where(out, zero, value)
+                coef[e, :, r, :] = value
+                total = total + jnp.abs(value)
+            diag[:, r, :] = total
+            return carry
+
+        lax.fori_loop(0, tiles, coef_tile, 0)
+
+        def gather(refs, t, acc):
+            near = near_of(refs, t)
+            r = rows_of(t)
+            for e, (vector, comp, sign) in enumerate(OFFSETS):
+                acc = acc + coef[e, :, r, :] * near(vector)
+            return acc
+
+        a_refs = (va, vap, vam)
+        b_refs = (vb, vbp, vbm)
+
+        def inside_tile(t, carry):
+            r = rows_of(t)
+            part[:, r, :] = gather(a_refs, t, src_ref[:, r, :])
+            return carry
+
+        lax.fori_loop(0, tiles, inside_tile, 0)
+
+        arrive(0)
+
+        gid = getters(0, 0)
+        glp = getters(0, 1)
+
+        def tensor_get(k):
+            def of(which):
+                def get(*args):
+                    code = gid[which](*args)
+                    return lookup(code, [k])[0] * jnp.exp(glp[which](*args))
+                return get
+            return of(0), of(1), of(2)
+
+        gets = {k: tensor_get(k) for k in range(6)}
+        rim_x = {}
+        for side, sx in ((0, -1), (1, 1)):
+            row = 8 if sx == -1 else top - 1
+            own = {k: ten[k, 1 : cz + 1, row, :] for k in (1, 3, 5)}
+            values = [harmonic(own[1], near_x(gets[1], sx, "")[0])]
+            near = near_x(gets[3], sx, "z")
+            for dz, got, ok in ((1, near[1], sub_x < last), (-1, near[2], sub_x > 0)):
+                values.append(jnp.where(ok, 0.125 * (dz * sx) * (own[3] + got), zero))
+            near = near_x(gets[5], sx, "y")
+            for dy, got in ((1, near[1]), (-1, near[2])):
+                values.append(0.125 * (sx * dy) * (own[5] + got))
+            size = None
+            for j, value in enumerate(values):
+                rcx[side, j] = value
+                size = jnp.abs(value) if size is None else size + jnp.abs(value)
+            rim_x[sx] = size
+
+        code = ys1[0]
+        gain = jnp.exp(ys1[1])
+        own = {k: f * gain for k, f in zip((2, 4, 5), lookup(code, (2, 4, 5)))}
+        sy = jnp.where(even, jnp.float32(0.125), jnp.float32(-0.125))
+        values = [harmonic(own[2], near_y(gets[2], "")[0])]
+        near = near_y(gets[4], "z")
+        for dz, got, ok in ((1, near[1], sub_y < 2 * last), (-1, near[2], sub_y >= 2)):
+            values.append(jnp.where(ok, dz * sy * (own[4] + got), zero))
+        near = near_y(gets[5], "x")
+        for dx, got, ok in ((1, near[1], lane_y < LANES - 1), (-1, near[2], lane_y > 0)):
+            values.append(jnp.where(ok, dx * sy * (own[5] + got), zero))
+        size = None
+        for j, value in enumerate(values):
+            rcy[j] = value
+            size = jnp.abs(value) if size is None else size + jnp.abs(value)
+        pack[0 : 2 * cz, :] = size
+        pack_sides(gets[4])
+        turned = pack[...].T
+        rim_z = {}
+        for side, sz in ((0, -1), (1, 1)):
+            z = 1 if sz == -1 else cz
+            own = {k: ten[k, z, 8:top, :] for k in (0, 3, 4)}
+            values = [harmonic(own[0], near_z(gets[0], sz, "", None)[0])]
+            near = near_z(gets[3], sz, "x", None)
+            for dx, got in ((1, near[1]), (-1, near[2])):
+                values.append(0.125 * (sz * dx) * (own[3] + got))
+            near = near_z(gets[4], sz, "y", turned)
+            for dy, got in ((1, near[1]), (-1, near[2])):
+                values.append(0.125 * (sz * dy) * (own[4] + got))
+            size = None
+            for j, value in enumerate(values):
+                rcz[side, j] = value
+                size = jnp.abs(value) if size is None else size + jnp.abs(value)
+            rim_z[sz] = size
+        spread(robin, False, turned, lambda sx: rim_x[sx], lambda sz: rim_z[sz])
+
+        def scale_tile(t, carry):
+            r = rows_of(t)
+            rim = robin[:, r, :]
+            total = diag[:, r, :] + rim
             rim = ROBIN * rim
             diag[:, r, :] = total
             robin[:, r, :] = rim
             inv[:, r, :] = 1.0 / (total + rim)
             return carry
 
-        lax.fori_loop(0, tiles, coef_tile, 0)
-
-        def gather(refs, t, acc):
-            near = near_of(refs, t)
-            r = rows_of(t)
-            for e, (vector, comp, sign) in enumerate(OFFSETS):
-                acc = acc + coef[e, :, r, :] * near(vector)
-            return acc
-
-        a_refs = (va, vap, vam)
-        b_refs = (vb, vbp, vbm)
-
-        def first_sweep(t, carry):
+        lax.fori_loop(0, tiles, scale_tile, 0)
+
+        def weigh(weights, values):
+            out = None
+            for j, value in enumerate(values):
+                term = weights(j) * value
+                out = term if out is None else out + term
+            return out
+
+        def spread_pressure(dest, add, stage, q):
+            get = getters(stage, q)
+            pack[0 : 2 * cz, :] = weigh(lambda j: rcy[j], near_y(get, "zx"))
+            pack_sides(get)
+            turned = pack[...].T
+            spread(
+                dest, add, turned,
+                lambda sx: weigh(lambda j: rcx[(sx + 1) // 2, j], near_x(get, sx, "zy")),
+                lambda sz: weigh(lambda j: rcz[(sz + 1) // 2, j], near_z(get, sz, "xy", turned)),
+            )
+
+        def first_tile(t, carry):
             r = rows_of(t)
             mid = rows_of(t + 1)
-            steady = src_ref[:, r, :] + robin[:, r, :] * va[1 : cz + 1, mid, :]
-            base[:, r, :] = steady
-            u = gather(a_refs, t, steady) * inv[:, r, :]
+            fixed = base[:, r, :] + robin[:, r, :] * va[1 : cz + 1, mid, :]
+            u = (fixed + part[:, r, :]) * inv[:, r, :]
+            base[:, r, :] = fixed + src_ref[:, r, :]
+            ahead, behind = turn(u)
             vb[1 : cz + 1, mid, :] = u
-            ahead, behind = shift_pair(u, vh[1 : cz + 1, mid, :])
             vbp[1 : cz + 1, mid, :] = ahead
             vbm[1 : cz + 1, mid, :] = behind
             return carry
 
-        def last_sweep(t, carry):
+        def second_tile(t, carry):
             r = rows_of(t)
             mid = rows_of(t + 1)
             u = gather(b_refs, t, base[:, r, :]) * inv[:, r, :]
+            ahead, behind = turn(u)
             va[1 : cz + 1, mid, :] = u
+            vap[1 : cz + 1, mid, :] = ahead
+            vam[1 : cz + 1, mid, :] = behind
+            return carry
+
+        def residual_tile(t, carry):
+            r = rows_of(t)
+            value = va[1 : cz + 1, rows_of(t + 1), :]
+            out_ref[:, r, :] = value
+            applied = src_ref[:, r, :] - diag[:, r, :] * value
+            res_ref[:, r, :] = gather(a_refs, t, applied)
             return carry
 
         for step in range(ITERS):
-            load_halo(step, 2 if step == 0 else 0)
-            lax.fori_loop(0, tiles, first_sweep, 0)
-            lax.fori_loop(0, tiles, last_sweep, 0)
+            spread_pressure(base, False, step, 2 if step == 0 else 0)
+            lax.fori_loop(0, tiles, first_tile, 0)
+            lax.fori_loop(0, tiles, second_tile, 0)
             pack_faces(
                 step + 1, 0,
                 lambda z: va[z + 1, 8:top, :],
@@ -399,18 +518,11 @@
             )
             start(step + 1)
             if step == ITERS - 1:
-                out_ref[...] = va[1 : cz + 1, 8:top, :]
+                lax.fori_loop(0, tiles, residual_tile, 0)
+            else:
+                lax.fori_loop(0, tiles, inside_tile, 0)
             arrive(step + 1)
-        load_halo(ITERS, 0)
-
-        def residual_tile(t, carry):
-            r = rows_of(t)
-            mid = rows_of(t + 1)
-            applied = src_ref[:, r, :] - diag[:, r, :] * va[1 : cz + 1, mid, :]
-            res_ref[:, r, :] = gather(a_refs, t, applied)
-            return carry
-
-        lax.fori_loop(0, tiles, residual_tile, 0)
+        spread_pressure(res_ref, True, ITERS, 0)
 
         for stage in range(ITERS + 1):
             for d in DIRS:
@@ -453,13 +565,17 @@
                 pltpu.VMEM((6,) + padded, f32),
                 pltpu.VMEM((3,) + padded, f32),
                 pltpu.VMEM((3,) + padded, f32),
-                pltpu.VMEM((3,) + padded, f32),
-                pltpu.VMEM(shape, f32),
             ]
-            + [pltpu.VMEM(padded, f32)] * 7
+            + [pltpu.VMEM(padded, f32)] * 6
             + [pltpu.VMEM((len(OFFSETS),) + shape, f32)]
-            + [pltpu.VMEM(shape, f32)] * 4
-            + [pltpu.VMEM((cx, cy), f32)]
+            + [pltpu.VMEM(shape, f32)] * 5
+            + [
+                pltpu.VMEM((cx, cy), f32),
+                pltpu.VMEM((cx + 16, cy), f32),
+                pltpu.VMEM((2, 5, cz, cy), f32),
+                pltpu.VMEM((5, 2 * cz, cx), f32),
+                pltpu.VMEM((2, 5, cx, cy), f32),
+            ]
             + exchange(3)
             + exchange(1)
             + exchange(1)
@@ -468,10 +584,10 @@
                 pltpu.SemaphoreType.DMA((ITERS + 1, len(DIRS))),
             ],
             compiler_params=pltpu.CompilerParams(
-                collective_id=0, has_side_effects=True, vmem_limit_bytes=60 * 1024 * 1024
+                collective_id=0, has_side_effects=True, vmem_limit_bytes=40 * 1024 * 1024
             ),
             name="schwarz",
-        )(rock_ids, log_perm, rock_diagonal, rock_shear, rock_storage, source, pressure_start)
+        )(rock_ids, log_perm, rock_diagonal.T, rock_shear.T, rock_storage, source, pressure_start)
 
     block = P("gz", "gx", "gy")
     return jax.shard_map(

time: 48.2 us -> 40.2 us (0.83)
  Pallas kernels: 42.6 us -> 32 us
  local copies, waits for them, and re-layouts: 4.76 us -> 7.1 us
    pallas_call x1, Pallas kernels: 42.6 us -> 32 us  [per_device(): pl.pallas_call(make_kernel(sizes, shape, classes), out_shape=(jax.ShapeDt...]
    unnamed x8 -> x16, local copies, waits for them, and re-layouts: 4.76 us -> 7.1 us
where the time goes in v1:
time: 40.2 us; the launch traced here: 39.8 us
  Pallas kernels  32 us (80%)
  local copies, waits for them, and re-layouts  7.1 us (18%)
  between operations  0.66 us (2%)
    pallas_call x1, Pallas kernels, per_device(): pl.pallas_call(make_kernel(sizes, shape, classes), out_shape=(jax.ShapeDt...  32 us
    unnamed x16, local copies, waits for them, and re-layouts  7.1 us

profile of v1, /device:TPU:0, one launch (start us, length us, event | category | flops | bytes accessed | tf_op | source)
XLA Modules:
  0.0 39.8 jit_solution(8911781417264193996)
XLA Ops:
  0.6 0.0 copy-start.4
  0.6 0.0 copy-start.6
  0.7 0.7 %copy-done.4 = f32[8,3]{0,1:T(4,128)S(1)} copy-done((f32[8,3]{0,1:T(4,128)S(1)}, f32[8,3]{0,1:T(4,128)}, u32[]{:S(2)}) %copy-start.4) | copy-done | bytes 120
  1.3 0.0 copy-done.6
  1.3 0.0 copy-start
  1.3 1.0 %copy-done = s32[8,128,128]{2,1,0:T(8,128)S(1)} copy-done((s32[8,128,128]{2,1,0:T(8,128)S(1)}, s32[8,128,128]{2,1,0:T(8,128)}, u32[]{:S(2)}) %copy-start) | copy-done | bytes 524312
  2.4 0.0 copy-start.1
  2.4 1.0 %copy-done.1 = f32[8,128,128]{2,1,0:T(8,128)S(1)} copy-done((f32[8,128,128]{2,1,0:T(8,128)S(1)}, f32[8,128,128]{2,1,0:T(8,128)}, u32[]{:S(2)}) %copy-start.1) | copy-done | bytes 524312
  3.4 0.0 copy-start.2
  3.4 1.0 %copy-done.2 = f32[8,128,128]{2,1,0:T(8,128)S(1)} copy-done((f32[8,128,128]{2,1,0:T(8,128)S(1)}, f32[8,128,128]{2,1,0:T(8,128)}, u32[]{:S(2)}) %copy-start.2) | copy-done | bytes 524312
  4.4 0.0 copy-start.3
  4.4 1.0 %copy-done.3 = f32[8,128,128]{2,1,0:T(8,128)S(1)} copy-done((f32[8,128,128]{2,1,0:T(8,128)S(1)}, f32[8,128,128]{2,1,0:T(8,128)}, u32[]{:S(2)}) %copy-start.3) | copy-done | bytes 524312
  5.5 0.0 copy-start.5
  5.5 0.7 %copy-done.5 = f32[8,3]{0,1:T(4,128)S(1)} copy-done((f32[8,3]{0,1:T(4,128)S(1)}, f32[8,3]{0,1:T(4,128)}, u32[]{:S(2)}) %copy-start.5) | copy-done | bytes 120
  6.2 32.0 %schwarz.1 = (f32[8,128,128]{2,1,0:T(8,128)S(1)}, f32[8,128,128]{2,1,0:T(8,128)S(1)}) custom-call(s32[8,128,128]{2,1,0:T(8,128)S(1)} %copy-done, f32[8,128,128]{2,1,0:T(8,128)S(1)} %copy-done.1, f32[3,8]{1,0:T(4,128)S(1)} %bitcast.2, f32[3,8]{1,0:T(4,128)S(1)} %bitcast.3, f32[8]{0:T(128)S(1)} %copy-done.6, f32[8,128,128]{2,1,0:T(8,128)S(1)} %copy-done.2, ...), custom_call_target="tpu_custom_call" | custom-call | tf_op jit(solution)/shard_map/schwarz/pallas_call | solution.py:558
  38.2 0.8 %copy.11 = f32[8,128,128]{2,1,0:T(8,128)} copy(f32[8,128,128]{2,1,0:T(8,128)S(1)} %get-tuple-element.4) | data formatting | bytes 1048576
  39.0 0.8 %copy.12 = f32[8,128,128]{2,1,0:T(8,128)} copy(f32[8,128,128]{2,1,0:T(8,128)S(1)} %get-tuple-element.5) | data formatting | bytes 1048576
Async XLA Ops:
  0.6 0.7 %copy-start.4 = (f32[8,3]{0,1:T(4,128)S(1)}, f32[8,3]{0,1:T(4,128)}, u32[]{:S(2)}) copy-start(f32[8,3]{0,1:T(4,128)} %param.9) | copy-start | bytes 292
  0.6 0.7 %copy-start.6 = (f32[8]{0:T(128)S(1)}, f32[8]{0:T(128)}, u32[]{:S(2)}) copy-start(f32[8]{0:T(128)} %sto_ref.1) | copy-start | bytes 100
  1.3 1.0 %copy-start = (s32[8,128,128]{2,1,0:T(8,128)S(1)}, s32[8,128,128]{2,1,0:T(8,128)}, u32[]{:S(2)}) copy-start(s32[8,128,128]{2,1,0:T(8,128)} %ids_ref.1) | copy-start | bytes 1572868
  2.4 1.0 %copy-start.1 = (f32[8,128,128]{2,1,0:T(8,128)S(1)}, f32[8,128,128]{2,1,0:T(8,128)}, u32[]{:S(2)}) copy-start(f32[8,128,128]{2,1,0:T(8,128)} %lp_ref.1) | copy-start | bytes 1572868
  3.4 1.0 %copy-start.2 = (f32[8,128,128]{2,1,0:T(8,128)S(1)}, f32[8,128,128]{2,1,0:T(8,128)}, u32[]{:S(2)}) copy-start(f32[8,128,128]{2,1,0:T(8,128)} %src_ref.1) | copy-start | bytes 1572868
  4.4 1.0 %copy-start.3 = (f32[8,128,128]{2,1,0:T(8,128)S(1)}, f32[8,128,128]{2,1,0:T(8,128)}, u32[]{:S(2)}) copy-start(f32[8,128,128]{2,1,0:T(8,128)} %p_ref.1) | copy-start | bytes 1572868
  5.5 0.7 %copy-start.5 = (f32[8,3]{0,1:T(4,128)S(1)}, f32[8,3]{0,1:T(4,128)}, u32[]{:S(2)}) copy-start(f32[8,3]{0,1:T(4,128)} %param.10) | copy-start | bytes 292

commit v2 on v1

--- a/solution.py
+++ b/solution.py
@@ -40,6 +40,8 @@
 X_SLOT = {d: i for i, d in enumerate(X_DIRS)}
 Y_SLOT = {d: i for i, d in enumerate(Y_DIRS)}
 Z_SLOT = {d: i for i, d in enumerate(Z_DIRS)}
+X_FIRST = sorted(X_DIRS, key=lambda d: -abs(d[2]))
+YZ_DIRS = Y_DIRS + Z_DIRS
 
 
 def make_kernel(sizes, shape, classes):
@@ -49,8 +51,8 @@
     last = cz - 1
 
     def kernel(
-        ids_ref, lp_ref, dia_ref, she_ref, sto_ref, src_ref, p_ref,
-        out_ref, res_ref,
+        ids_hbm, lp_hbm, dia_ref, she_ref, sto_ref, src_hbm, p_hbm,
+        out_hbm, res_hbm,
         tab, ten, ten_p, ten_m,
         va, vap, vam, vb, vbp, vbm,
         coef, diag, robin, inv, base, part, pack, zpad,
@@ -58,8 +60,17 @@
         zs1, xs1, ys1, zl1, xl1, yl1,
         zs2, xs2, ys2, zl2, xl2, yl2,
         zs3, xs3, ys3, zl3, xl3, yl3,
+        ids_ref, lp_ref, src_ref, p_ref, res_ref, load_sem,
         send_sem, recv_sem,
     ):
+        loads = [
+            pltpu.make_async_copy(a, b, load_sem.at[i])
+            for i, (a, b) in enumerate(
+                ((ids_hbm, ids_ref), (lp_hbm, lp_ref), (p_hbm, p_ref), (src_hbm, src_ref))
+            )
+        ]
+        for load in loads:
+            load.start()
         here = [lax.axis_index(a) for a in AXES]
 
         def exists(d):
@@ -105,8 +116,9 @@
             zs, xs, ys = stages[stage][:3]
             for side, z in ((0, 0), (1, last)):
                 zs[side, q] = plane(z)
-            for side, x in ((0, 0), (1, cx - 1)):
-                xs[side, q] = row(x)
+            if row is not None:
+                for side, x in ((0, 0), (1, cx - 1)):
+                    xs[side, q] = row(x)
             mixed = jnp.zeros((cx, LANES), jnp.float32)
             for z in range(cz):
                 moved = pltpu.roll(plane(z), 2 * z + 1, 1)
@@ -131,8 +143,8 @@
         def opposite(d):
             return tuple(-c for c in d)
 
-        def start(stage):
-            for d in reversed(DIRS):
+        def start(stage, dirs):
+            for d in dirs:
                 @pl.when(there[d])
                 def _(d=d):
                     copy_of(stage, d).start()
@@ -239,6 +251,9 @@
                     dest[z] = got
             for sx, row in ((-1, 0), (1, cx - 1)):
                 dest[:, row, :] += of_x(sx)
+
+        for load in loads[:3]:
+            load.wait()
 
         pack_faces(
             0, 0,
@@ -298,10 +313,10 @@
             vam[1 : cz + 1, out, :] = behind
             return carry
 
-        lax.fori_loop(0, tiles, tensor_tile, 0)
+        lax.fori_loop(0, tiles, tensor_tile, 0, unroll=2)
 
         pl.semaphore_wait(barrier, expected)
-        start(0)
+        start(0, X_FIRST + YZ_DIRS)
 
         def near_of(refs, t):
             plain, plus, minus = refs
@@ -373,12 +388,14 @@
         a_refs = (va, vap, vam)
         b_refs = (vb, vbp, vbm)
 
+        loads[3].wait()
+
         def inside_tile(t, carry):
             r = rows_of(t)
             part[:, r, :] = gather(a_refs, t, src_ref[:, r, :])
             return carry
 
-        lax.fori_loop(0, tiles, inside_tile, 0)
+        lax.fori_loop(0, tiles, inside_tile, 0, unroll=2)
 
         arrive(0)
 
@@ -457,7 +474,7 @@
             inv[:, r, :] = 1.0 / (total + rim)
             return carry
 
-        lax.fori_loop(0, tiles, scale_tile, 0)
+        lax.fori_loop(0, tiles, scale_tile, 0, unroll=2)
 
         def weigh(weights, values):
             out = None
@@ -502,27 +519,35 @@
         def residual_tile(t, carry):
             r = rows_of(t)
             value = va[1 : cz + 1, rows_of(t + 1), :]
-            out_ref[:, r, :] = value
             applied = src_ref[:, r, :] - diag[:, r, :] * value
             res_ref[:, r, :] = gather(a_refs, t, applied)
             return carry
 
         for step in range(ITERS):
             spread_pressure(base, False, step, 2 if step == 0 else 0)
-            lax.fori_loop(0, tiles, first_tile, 0)
-            lax.fori_loop(0, tiles, second_tile, 0)
-            pack_faces(
-                step + 1, 0,
-                lambda z: va[z + 1, 8:top, :],
-                lambda x: va[1 : cz + 1, 8 + x, :],
-            )
-            start(step + 1)
+            lax.fori_loop(0, tiles, first_tile, 0, unroll=2)
+            lax.fori_loop(0, 2, lambda i, c: second_tile(i * (tiles - 1), c), 0, unroll=2)
+            for side, x in ((0, 8), (1, top - 1)):
+                stages[step + 1][1][side, 0] = va[1 : cz + 1, x, :]
+            start(step + 1, X_FIRST)
+            lax.fori_loop(1, tiles - 1, second_tile, 0, unroll=2)
+            pack_faces(step + 1, 0, lambda z: va[z + 1, 8:top, :], None)
+            start(step + 1, YZ_DIRS)
             if step == ITERS - 1:
-                lax.fori_loop(0, tiles, residual_tile, 0)
+                put_out = pltpu.make_async_copy(
+                    va.at[1 : cz + 1, 8:top, :], out_hbm, load_sem.at[4]
+                )
+                put_out.start()
+            if step == ITERS - 1:
+                lax.fori_loop(0, tiles, residual_tile, 0, unroll=2)
             else:
-                lax.fori_loop(0, tiles, inside_tile, 0)
+                lax.fori_loop(0, tiles, inside_tile, 0, unroll=2)
             arrive(step + 1)
         spread_pressure(res_ref, True, ITERS, 0)
+        put_res = pltpu.make_async_copy(res_ref, res_hbm, load_sem.at[5])
+        put_res.start()
+        put_out.wait()
+        put_res.wait()
 
         for stage in range(ITERS + 1):
             for d in DIRS:
@@ -553,13 +578,13 @@
                 pltpu.VMEM((len(Y_DIRS), nq, 2 * cz, cx), f32),
             ]
 
-        vmem = pl.BlockSpec(memory_space=pltpu.VMEM)
+        hbm = pl.BlockSpec(memory_space=pltpu.HBM)
         smem = pl.BlockSpec(memory_space=pltpu.SMEM)
         return pl.pallas_call(
             make_kernel(sizes, shape, classes),
             out_shape=(jax.ShapeDtypeStruct(shape, f32), jax.ShapeDtypeStruct(shape, f32)),
-            in_specs=[vmem, vmem, smem, smem, smem, vmem, vmem],
-            out_specs=(vmem, vmem),
+            in_specs=[hbm, hbm, smem, smem, smem, hbm, hbm],
+            out_specs=(hbm, hbm),
             scratch_shapes=[
                 pltpu.VMEM((7, classes, 8, cy), f32),
                 pltpu.VMEM((6,) + padded, f32),
@@ -579,12 +604,15 @@
             + exchange(3)
             + exchange(1)
             + exchange(1)
+            + [pltpu.VMEM(shape, jnp.int32)]
+            + [pltpu.VMEM(shape, f32)] * 4
             + [
+                pltpu.SemaphoreType.DMA((6,)),
                 pltpu.SemaphoreType.DMA((ITERS + 1, len(DIRS))),
                 pltpu.SemaphoreType.DMA((ITERS + 1, len(DIRS))),
             ],
             compiler_params=pltpu.CompilerParams(
-                collective_id=0, has_side_effects=True, vmem_limit_bytes=40 * 1024 * 1024
+                collective_id=0, has_side_effects=True, vmem_limit_bytes=61440 * 1024
             ),
             name="schwarz",
         )(rock_ids, log_perm, rock_diagonal.T, rock_shear.T, rock_storage, source, pressure_start)

time: 40.2 us -> 31.3 us (0.78)
  local copies, waits for them, and re-layouts: 7.1 us -> 2.73 us
  Pallas kernels: 32 us -> 27.7 us
    unnamed x16 -> x4, local copies, waits for them, and re-layouts: 7.1 us -> 2.73 us
    pallas_call x1, Pallas kernels: 32 us -> 27.7 us  [per_device(): pl.pallas_call(make_kernel(sizes, shape, classes), out_shape=(jax.ShapeDt...]
where the time goes in v2:
time: 31.3 us; the launch traced here: 31.1 us
  Pallas kernels  27.7 us (88%)
  local copies, waits for them, and re-layouts  2.73 us (9%)
  between operations  0.65 us (2%)
    pallas_call x1, Pallas kernels, per_device(): pl.pallas_call(make_kernel(sizes, shape, classes), out_shape=(jax.ShapeDt...  27.7 us
    unnamed x4, local copies, waits for them, and re-layouts  2.73 us

profile of v2, /device:TPU:0, one launch (start us, length us, event | category | flops | bytes accessed | tf_op | source)
XLA Modules:
  0.0 31.1 jit_solution(15681399951110566959)
XLA Ops:
  0.6 27.7 %schwarz.1 = (f32[8,128,128]{2,1,0:T(8,128)}, f32[8,128,128]{2,1,0:T(8,128)}) custom-call(s32[8,128,128]{2,1,0:T(8,128)} %ids_hbm.1, f32[8,128,128]{2,1,0:T(8,128)} %lp_hbm.1, f32[3,8]{1,0:T(4,128)} %bitcast.2, f32[3,8]{1,0:T(4,128)} %bitcast.3, f32[8]{0:T(128)} %sto_ref.1, f32[8,128,128]{2,1,0:T(8,128)} %src_hbm.1, f32[8,128,128]{2,1,0:T(8,128)} %p_hbm.1), custom_call_target="tpu_custom_call" | custom-call | tf_op jit(solution)/shard_map/schwarz/pallas_call | solution.py:583
  28.4 0.0 copy-start
  28.4 1.9 %copy.11 = f32[8,128,128]{2,1,0:T(8,128)} copy(f32[8,128,128]{2,1,0:T(8,128)} %get-tuple-element.4) | data formatting | bytes 1048576
  30.3 0.0 copy-done
  30.3 0.8 %copy.12 = f32[8,128,128]{2,1,0:T(8,128)} copy(f32[8,128,128]{2,1,0:T(8,128)S(1)} %copy-done) | data formatting | bytes 1048576
Async XLA Ops:
  28.4 1.9 %copy-start = (f32[8,128,128]{2,1,0:T(8,128)S(1)}, f32[8,128,128]{2,1,0:T(8,128)}, u32[]{:S(2)}) copy-start(f32[8,128,128]{2,1,0:T(8,128)} %get-tuple-element.5) | copy-start | bytes 1572868

commit v3 on v2

--- a/solution.py
+++ b/solution.py
@@ -395,7 +395,7 @@
             part[:, r, :] = gather(a_refs, t, src_ref[:, r, :])
             return carry
 
-        lax.fori_loop(0, tiles, inside_tile, 0, unroll=2)
+        lax.fori_loop(0, tiles, inside_tile, 0, unroll=4)
 
         arrive(0)
 
@@ -474,7 +474,7 @@
             inv[:, r, :] = 1.0 / (total + rim)
             return carry
 
-        lax.fori_loop(0, tiles, scale_tile, 0, unroll=2)
+        lax.fori_loop(0, tiles, scale_tile, 0, unroll=4)
 
         def weigh(weights, values):
             out = None
@@ -525,7 +525,7 @@
 
         for step in range(ITERS):
             spread_pressure(base, False, step, 2 if step == 0 else 0)
-            lax.fori_loop(0, tiles, first_tile, 0, unroll=2)
+            lax.fori_loop(0, tiles, first_tile, 0, unroll=4)
             lax.fori_loop(0, 2, lambda i, c: second_tile(i * (tiles - 1), c), 0, unroll=2)
             for side, x in ((0, 8), (1, top - 1)):
                 stages[step + 1][1][side, 0] = va[1 : cz + 1, x, :]
@@ -539,9 +539,9 @@
                 )
                 put_out.start()
             if step == ITERS - 1:
-                lax.fori_loop(0, tiles, residual_tile, 0, unroll=2)
+                lax.fori_loop(0, tiles, residual_tile, 0, unroll=4)
             else:
-                lax.fori_loop(0, tiles, inside_tile, 0, unroll=2)
+                lax.fori_loop(0, tiles, inside_tile, 0, unroll=4)
             arrive(step + 1)
         spread_pressure(res_ref, True, ITERS, 0)
         put_res = pltpu.make_async_copy(res_ref, res_hbm, load_sem.at[5])

time: 31.3 us -> 30.6 us (0.978)
  Pallas kernels: 27.7 us -> 27 us
    pallas_call x1, Pallas kernels: 27.7 us -> 27 us  [per_device(): pl.pallas_call(make_kernel(sizes, shape, classes), out_shape=(jax.ShapeDt...]
where the time goes in v3:
time: 30.6 us; the launch traced here: 30.4 us
  Pallas kernels  27 us (88%)
  local copies, waits for them, and re-layouts  2.73 us (9%)
  between operations  0.65 us (2%)
    pallas_call x1, Pallas kernels, per_device(): pl.pallas_call(make_kernel(sizes, shape, classes), out_shape=(jax.ShapeDt...  27 us
    unnamed x4, local copies, waits for them, and re-layouts  2.73 us

profile of v3, /device:TPU:0, one launch (start us, length us, event | category | flops | bytes accessed | tf_op | source)
XLA Modules:
  0.0 30.4 jit_solution(13301991589920364278)
XLA Ops:
  0.6 27.0 %schwarz.1 = (f32[8,128,128]{2,1,0:T(8,128)}, f32[8,128,128]{2,1,0:T(8,128)}) custom-call(s32[8,128,128]{2,1,0:T(8,128)} %ids_hbm.1, f32[8,128,128]{2,1,0:T(8,128)} %lp_hbm.1, f32[3,8]{1,0:T(4,128)} %bitcast.2, f32[3,8]{1,0:T(4,128)} %bitcast.3, f32[8]{0:T(128)} %sto_ref.1, f32[8,128,128]{2,1,0:T(8,128)} %src_hbm.1, f32[8,128,128]{2,1,0:T(8,128)} %p_hbm.1), custom_call_target="tpu_custom_call" | custom-call | tf_op jit(solution)/shard_map/schwarz/pallas_call | solution.py:583
  27.7 0.0 copy-start
  27.7 1.9 %copy.11 = f32[8,128,128]{2,1,0:T(8,128)} copy(f32[8,128,128]{2,1,0:T(8,128)} %get-tuple-element.4) | data formatting | bytes 1048576
  29.6 0.0 copy-done
  29.6 0.8 %copy.12 = f32[8,128,128]{2,1,0:T(8,128)} copy(f32[8,128,128]{2,1,0:T(8,128)S(1)} %copy-done) | data formatting | bytes 1048576
Async XLA Ops:
  27.7 1.9 %copy-start = (f32[8,128,128]{2,1,0:T(8,128)S(1)}, f32[8,128,128]{2,1,0:T(8,128)}, u32[]{:S(2)}) copy-start(f32[8,128,128]{2,1,0:T(8,128)} %get-tuple-element.5) | copy-start | bytes 1572868
